TPU v7x, 32 devices: a whole 2x2x4 slice. The times are simulated.
32 devices in a mesh: grp: 2 (over x), wide: 16 (over z, y, core).
Axes of the slice: x: 2, y: 2, z: 4, core: 2. Of those that a mesh axis runs over, the one named last changes fastest.
Arguments:
- hidden: bfloat16 [32, 256, 8192], P(('grp', 'wide')), parts along dimension 0, may hold values from -6 to 6
- output_gradient: bfloat16 [32, 256, 8192], P(('grp', 'wide')), parts along dimension 0, may hold values from -6 to 6
- adapter_up_factor: bfloat16 [8192, 64], replicated, may hold values from -0.0625 to 0.0625
- first_moment_estimate: float32 [64, 8192], P(None, 'wide'), may hold values from -0.06 to 0.06
- second_moment_estimate: float32 [64, 8192], P(None, 'wide'), may hold values from 0.0001 to 0.01
- lengths: int32 [32], P(('grp', 'wide')), parts along dimension 0, may hold values from 32 to 256, as said below
- seeds: int32 [128], P('wide'), may hold values from 0 to 16777215
Outputs:
- features: float32 [32, 4096], P(('grp', 'wide')), parts along dimension 0
There are 2 independent parts, one for each index of `grp`. A program takes and returns all parts, laid end to end along the dimension named above; an argument that names none is the same for every part. Nothing has to cross between parts.
Inputs may be any that keep to these rules, and one draw needn't show every extreme that they name: `lengths`: some sequence has exactly 256 live tokens and some has 32.
All inputs are finite; a program needn't handle non-finite values.
Results may differ from a plain program's by a relative error of at most 0.0039.
Values may be sent and summed in bfloat16 or wider, within the bound.
No kernel may reach another device: no remote copies, remote signals or barrier semaphores. Data moves between devices by JAX's collectives and lax.ppermute only.
A program may use at most 384 MiB of HBM per device.

v0:
```python
import jax
import jax.numpy as jnp
from jax import lax
from jax.sharding import PartitionSpec as P

K = 4096
CB = 64
RB = 8


def mix_bits(hashed):
    for turn in range(2):
        hashed = hashed & 2147483647
        hashed = hashed ^ jnp.right_shift(hashed, 16)
        hashed = hashed * 73244475
    hashed = hashed & 2147483647
    hashed = hashed ^ jnp.right_shift(hashed, 16)
    return hashed


def build_signs(rank_rows, own_cols, seeds):
    col_blocks = own_cols // CB
    row_groups = rank_rows // RB
    row_ids = lax.broadcasted_iota(jnp.int32, (RB, CB, K), 0)
    col_ids = lax.broadcasted_iota(jnp.int32, (RB, CB, K), 1)
    feat_ids = lax.broadcasted_iota(jnp.int32, (RB, CB, K), 2)

    def fill_step(loop_index, table):
        loop_index = loop_index.astype(jnp.int32)
        col_pos = loop_index // row_groups
        grp_pos = loop_index % row_groups
        param_ids = (grp_pos * RB + row_ids) * CB + col_ids
        hashed = mix_bits(param_ids * 1000003 + feat_ids * 7919 + seeds[col_pos])
        block = (1 - 2 * (hashed & 1)).astype(jnp.bfloat16)
        return lax.dynamic_update_slice(table, block, (grp_pos * RB, col_pos * CB, jnp.int32(0)))

    table = jnp.zeros((rank_rows, own_cols, K), jnp.bfloat16)
    table = lax.fori_loop(0, col_blocks * row_groups, fill_step, table)
    return table.reshape(rank_rows * own_cols, K)


def shards(
    hidden,
    output_gradient,
    adapter_up_factor,
    first_moment_estimate,
    second_moment_estimate,
    lengths,
    seeds,
):
    own_seqs, tok_slots = (hidden.shape[0], hidden.shape[1])
    rank_reduced = jnp.einsum(
        "nuk,kv->nuv", output_gradient, adapter_up_factor, preferred_element_type=jnp.float32
    )
    live_mask = lax.broadcasted_iota(jnp.int32, (own_seqs, tok_slots), 1) < lengths[:, None]
    rank_reduced = jnp.where(live_mask[:, :, None], rank_reduced, 0.0).astype(jnp.bfloat16)
    summed = jnp.einsum("str,std->srd", rank_reduced, hidden, preferred_element_type=jnp.float32)
    seq_grad = (summed / lengths.astype(jnp.float32)[:, None, None]).astype(jnp.bfloat16)
    regrouped = lax.all_to_all(seq_grad, "wide", split_axis=2, concat_axis=0, tiled=True)
    grad_full = regrouped.astype(jnp.float32)
    first_new = 0.9 * first_moment_estimate[None] + 0.1 * grad_full
    second_new = 0.999 * second_moment_estimate[None] + 0.001 * grad_full * grad_full
    update = (first_new / (jnp.sqrt(second_new) + 1e-08)).astype(jnp.bfloat16)
    all_seqs, rank_rows, own_cols = update.shape
    flat_update = update.reshape(all_seqs, rank_rows * own_cols)
    signs = build_signs(rank_rows, own_cols, seeds)
    partial_value = jnp.dot(flat_update, signs, preferred_element_type=jnp.float32)
    totals = lax.psum(partial_value, "wide")
    own_rows = lax.dynamic_slice_in_dim(totals, lax.axis_index("wide") * own_seqs, own_seqs, 0)
    return own_rows * lax.rsqrt(jnp.mean(own_rows * own_rows, axis=1, keepdims=True) + 1e-06)


def solution(mesh):
    placed = (
        P(("grp", "wide"), None, None),
        P(("grp", "wide"), None, None),
        P(),
        P(None, "wide"),
        P(None, "wide"),
        P(("grp", "wide")),
        P("wide"),
    )
    return jax.shard_map(
        shards, mesh=mesh, in_specs=placed, out_specs=P(("grp", "wide"), None), check_vma=False
    )
```

profile of v0, /device:TPU:0, one launch (start us, length us, event | category | flops | bytes accessed | tf_op | source)
XLA Modules:
  0.0 859.6 jit_solution(11713822607061688417)
XLA Ops:
  21.7 45.2 %reduce.1 = bf16[8192,64]{1,0:T(8,128)(2,1)S(1)} reduce(bf16[8192,1,64]{2,1,0:T(2,128)(2,1)} %bitcast.44, bf16[]{:T(256)} %broadcast.116), dimensions={1}, to_apply=%bitcast.32.reduce_sub_computation | reduce | bytes 2097154
  69.1 7.4 all-to-all-start
  76.8 81.1 %broadcast_in_dim.23 = bf16[64,512,4096]{2,1,0:T(8,128)(2,1)} broadcast(bf16[]{:T(256)} %constant.173.clone.1), dimensions={} | broadcast | bytes 268435456 | tf_op jit(solution)/shard_map/broadcast_in_dim | solution.py:37
  157.9 496.9 %while.16 = (s32[]{:T(128)}, bf16[64,512,4096]{2,1,0:T(8,128)(2,1)}, s32[8]{0:T(128)S(1)}, s32[]{:T(128)}, s32[]{:T(128)}, /*index=5*/s32[]{:T(128)}, s32[]{:T(1...) while((s32[]{:T(128)}, bf16[64,512,4096]{2,1,0:T(8,128)(2,1)}, s32[8]{0:T(128)S(1)}, ...), condition=%wide.region_1.2_spmd.clone, body=%wide.region_0.1_spmd.clone.sunk | while | flops 46137368 | bytes 4195198 | solution.py:38
  158.5 7.2 fusion.57
  174.1 7.2 fusion.57
  181.9 7.2 fusion.57
  189.7 7.2 fusion.57
  205.2 7.2 fusion.57
  220.8 7.2 fusion.57
  236.3 7.2 fusion.57
  251.8 7.2 fusion.57
  267.4 7.2 fusion.57
  414.7 7.2 fusion.57
  430.2 7.2 fusion.57
  445.8 7.2 fusion.57
  476.9 7.2 fusion.57
  507.9 7.2 fusion.57
  601.0 7.2 fusion.57
  624.2 7.2 fusion.57
  639.8 7.2 fusion.57
  661.8 8.5 bitcast_convert_fusion
  673.6 84.2 %convolution_bitcast_fusion = f32[16,4096]{1,0:T(8,128)} fusion(bf16[64,512,4096]{2,1,0:T(8,128)(2,1)} %get-tuple-element.162, f32[1,64,16,512]{3,2,1,0:T(8,128)S(1)} %copy.9, f32[64,512]{1,0:T(8,128)S(1)} %get-tuple-element.179, f32[64,512]{1,0:T(8,128)S(1)} %get-tuple-element.180), kind=kOutput, calls=%fused_computation.26 | convolution fusion | flops 4299161600 | bytes 271056896 | tf_op jit(solution)/shard_map/dot_general | solution.py:67
  757.8 91.2 %all-reduce.2.cloned.1.call-done = f32[16,4096]{1,0:T(8,128)} async-done(((f32[16,4096]{1,0:T(8,128)}), f32[16,4096]{1,0:T(8,128)}) %all-reduce.2.cloned.1.call-update) | async-done | bytes 262160 | tf_op jit(solution)/shard_map/psum | solution.py:68
  (132 shorter events, 404.9 us)
Async XLA Ops:
  6.5 1.2 copy-start
  69.1 585.7 %all-to-all-start = ((bf16[16,2,16384]{2,1,0:T(2,128)(2,1)}), bf16[16,2,16384]{2,1,0:T(2,128)(2,1)S(1)}, u32[]{:S(2)}, u32[]{:S(2)}) async-start(bf16[16,2,16384]{2,1,0:T(2,128)(2,1)} %reshape.53), calls=%async_computation | async-start | bytes 2097152 | tf_op jit(solution)/shard_map/all_to_all | solution.py:59
  76.5 772.5 %all-reduce.2.cloned.1.call-start = ((), (), s32[]{:S(2)}) async-start(), calls=%async_computation.1 | async-start | bytes 524288 | tf_op jit(solution)/shard_map/psum | solution.py:68
  76.8 81.1 %copy-start.3 = (s32[8]{0:T(128)S(1)}, s32[8]{0:T(128)}, u32[]{:S(2)}) copy-start(s32[8]{0:T(128)} %param.15) | copy-start | bytes 100
  157.9 496.9 %copy-start.1 = (f32[64,512]{1,0:T(8,128)S(1)}, f32[64,512]{1,0:T(8,128)}, u32[]{:S(2)}) copy-start(f32[64,512]{1,0:T(8,128)} %param.13) | copy-start | bytes 393220
  157.9 496.9 %copy-start.2 = (f32[64,512]{1,0:T(8,128)S(1)}, f32[64,512]{1,0:T(8,128)}, u32[]{:S(2)}) copy-start(f32[64,512]{1,0:T(8,128)} %param.12) | copy-start | bytes 393220
Sparse Core Ops, SparseCore 0:
  758.0 91.0 all-reduce.1
where the time goes:
time: 861 us; the launch traced here: 860 us
  other arithmetic  515 us (60%)
  local copies, waits for them, and re-layouts  140 us (16%)
  waiting for transfers between devices  91.2 us (11%)
  matrix products  90.7 us (11%)
  between operations  14.9 us (2%)
    dynamic_update_slice x64, other arithmetic, fill_step(): lax.dynamic_update_slice(table, block, (grp_pos * RB, col_pos * CB, jnp.i...  459 us
    psum x1, waiting for transfers between devices, shards(): totals = lax.psum(partial_value, 'wide')  91.2 us
    dot_general x1, matrix products, shards(): jnp.dot(flat_update, signs, preferred_element_type=jnp.float32)  84.2 us
    broadcast_in_dim x1, local copies, waits for them, and re-layouts, build_signs(): table = jnp.zeros((rank_rows, own_cols, K), jnp.bfloat16)  81.1 us
    unnamed x1, other arithmetic  45.2 us
    dynamic_slice x64, local copies, waits for them, and re-layouts, fill_step(): hashed = mix_bits(param_ids * 1000003 + feat_ids * 7919 + seeds[col_pos])  38.1 us
  transfers between devices with their start and end apart: 2, of which 1 were waited for; matrix products, arithmetic and copies ran while one was open for 67% of the time, Pallas kernels for 0%

commit v1 on v0

--- a/solution.py
+++ b/solution.py
@@ -65,7 +65,7 @@
     flat_update = update.reshape(all_seqs, rank_rows * own_cols)
     signs = build_signs(rank_rows, own_cols, seeds)
     partial_value = jnp.dot(flat_update, signs, preferred_element_type=jnp.float32)
-    totals = lax.psum(partial_value, "wide")
+    totals = jnp.sum(lax.all_gather(partial_value, "wide"), axis=0)
     own_rows = lax.dynamic_slice_in_dim(totals, lax.axis_index("wide") * own_seqs, own_seqs, 0)
     return own_rows * lax.rsqrt(jnp.mean(own_rows * own_rows, axis=1, keepdims=True) + 1e-06)
 

time: 861 us -> 822 us (0.955)
  waiting for transfers between devices: 91.2 us -> 51.9 us
    psum x1 -> x0, waiting for transfers between devices: 91.2 us -> none  [shards(): totals = lax.psum(partial_value, 'wide')]
    all_gather x0 -> x1, waiting for transfers between devices: none -> 51.8 us  [shards(): totals = jnp.sum(lax.all_gather(partial_value, 'wide'), axis=0)]
  transfers between devices with their start and end apart: 2 -> 2, of which waited for: 1 -> 1; matrix products, arithmetic and copies ran while one was open for 67% -> 70% of each run, Pallas kernels for 0% -> 0%
where the time goes in v1:
time: 822 us; the launch traced here: 821 us
  other arithmetic  516 us (63%)
  local copies, waits for them, and re-layouts  140 us (17%)
  matrix products  90.7 us (11%)
  waiting for transfers between devices  51.9 us (6%)
  between operations  14.9 us (2%)
    dynamic_update_slice x64, other arithmetic, fill_step(): lax.dynamic_update_slice(table, block, (grp_pos * RB, col_pos * CB, jnp.i...  459 us
    dot_general x1, matrix products, shards(): jnp.dot(flat_update, signs, preferred_element_type=jnp.float32)  84.2 us
    broadcast_in_dim x1, local copies, waits for them, and re-layouts, build_signs(): table = jnp.zeros((rank_rows, own_cols, K), jnp.bfloat16)  81.1 us
    all_gather x1, waiting for transfers between devices, shards(): totals = jnp.sum(lax.all_gather(partial_value, 'wide'), axis=0)  51.8 us
    unnamed x1, other arithmetic  45.2 us
    dynamic_slice x64, local copies, waits for them, and re-layouts, fill_step(): hashed = mix_bits(param_ids * 1000003 + feat_ids * 7919 + seeds[col_pos])  38.1 us
  transfers between devices with their start and end apart: 2, of which 1 were waited for; matrix products, arithmetic and copies ran while one was open for 70% of the time, Pallas kernels for 0%

profile of v1, /device:TPU:0, one launch (start us, length us, event | category | flops | bytes accessed | tf_op | source)
XLA Modules:
  0.0 820.9 jit_solution(4725096752795277773)
XLA Ops:
  21.7 45.2 %reduce.1 = bf16[8192,64]{1,0:T(8,128)(2,1)S(1)} reduce(bf16[8192,1,64]{2,1,0:T(2,128)(2,1)} %bitcast.45, bf16[]{:T(256)} %broadcast.116), dimensions={1}, to_apply=%bitcast.33.reduce_sub_computation | reduce | bytes 2097154
  69.1 7.4 all-to-all-start
  76.8 81.1 %broadcast_in_dim.23 = bf16[64,512,4096]{2,1,0:T(8,128)(2,1)} broadcast(bf16[]{:T(256)} %constant.173.clone.1), dimensions={} | broadcast | bytes 268435456 | tf_op jit(solution)/shard_map/broadcast_in_dim | solution.py:37
  157.9 496.9 %while.16 = (s32[]{:T(128)}, bf16[64,512,4096]{2,1,0:T(8,128)(2,1)}, s32[8]{0:T(128)S(1)}, s32[]{:T(128)}, s32[]{:T(128)}, /*index=5*/s32[]{:T(128)}, s32[]{:T(1...) while((s32[]{:T(128)}, bf16[64,512,4096]{2,1,0:T(8,128)(2,1)}, s32[8]{0:T(128)S(1)}, ...), condition=%wide.region_1.2_spmd.clone, body=%wide.region_0.1_spmd.clone.sunk | while | flops 46137368 | bytes 4195198 | solution.py:38
  158.5 7.2 fusion.57
  174.1 7.2 fusion.57
  181.9 7.2 fusion.57
  189.7 7.2 fusion.57
  205.2 7.2 fusion.57
  220.8 7.2 fusion.57
  236.3 7.2 fusion.57
  251.8 7.2 fusion.57
  267.4 7.2 fusion.57
  414.7 7.2 fusion.57
  430.2 7.2 fusion.57
  445.8 7.2 fusion.57
  476.9 7.2 fusion.57
  507.9 7.2 fusion.57
  601.0 7.2 fusion.57
  624.2 7.2 fusion.57
  639.8 7.2 fusion.57
  661.8 8.5 %bitcast_convert_fusion = f32[1,64,8192]{1,0,2:T(1,128)} fusion(bf16[8192,1,64]{2,1,0:T(2,128)(2,1)} %reshape.55), kind=kLoop, calls=%fused_computation.56 | loop fusion | flops 524288 | bytes 3145728 | tf_op jit(solution)/shard_map/convert_element_type | solution.py:60
  673.6 84.2 %convolution_bitcast_fusion = f32[16,4096]{1,0:T(8,128)} fusion(bf16[64,512,4096]{2,1,0:T(8,128)(2,1)} %get-tuple-element.162, f32[1,64,16,512]{3,2,1,0:T(8,128)S(1)} %copy.9, f32[64,512]{1,0:T(8,128)S(1)} %get-tuple-element.179, f32[64,512]{1,0:T(8,128)S(1)} %get-tuple-element.180), kind=kOutput, calls=%fused_computation.26 | convolution fusion | flops 4299161600 | bytes 271056896 | tf_op jit(solution)/shard_map/dot_general | solution.py:67
  757.8 51.8 %all-gather.3.cloned.1.call-done = f32[256,4096]{1,0:T(8,128)} async-done(((f32[16,4096]{1,0:T(8,128)}), f32[256,4096]{1,0:T(8,128)}) %all-gather.3.cloned.1.call-update) | async-done | bytes 4194320 | tf_op jit(solution)/shard_map/all_gather | solution.py:68
  (133 shorter events, 405.5 us)
Async XLA Ops:
  6.5 1.2 copy-start
  69.1 585.7 %all-to-all-start = ((bf16[16,2,16384]{2,1,0:T(2,128)(2,1)}), bf16[16,2,16384]{2,1,0:T(2,128)(2,1)S(1)}, u32[]{:S(2)}, u32[]{:S(2)}) async-start(bf16[16,2,16384]{2,1,0:T(2,128)(2,1)} %reshape.54), calls=%async_computation | async-start | bytes 2097152 | tf_op jit(solution)/shard_map/all_to_all | solution.py:59
  76.5 733.1 %all-gather.3.cloned.1.call-start = ((), (), s32[]{:S(2)}) async-start(), calls=%async_computation.1 | async-start | bytes 4456448 | tf_op jit(solution)/shard_map/all_gather | solution.py:68
  76.8 81.1 %copy-start.3 = (s32[8]{0:T(128)S(1)}, s32[8]{0:T(128)}, u32[]{:S(2)}) copy-start(s32[8]{0:T(128)} %param.15) | copy-start | bytes 100
  157.9 496.9 %copy-start.1 = (f32[64,512]{1,0:T(8,128)S(1)}, f32[64,512]{1,0:T(8,128)}, u32[]{:S(2)}) copy-start(f32[64,512]{1,0:T(8,128)} %param.13) | copy-start | bytes 393220
  157.9 496.9 %copy-start.2 = (f32[64,512]{1,0:T(8,128)S(1)}, f32[64,512]{1,0:T(8,128)}, u32[]{:S(2)}) copy-start(f32[64,512]{1,0:T(8,128)} %param.12) | copy-start | bytes 393220
Sparse Core Ops, SparseCore 0:
  757.9 51.6 all-gather.2
